TPU v7x, 512 devices: a whole 4x8x8 slice. The times are simulated.
512 devices in a mesh: layer: 32 (over z_lo, x, core), dp: 8 (over y), mp: 2 (over z_hi).
Axes of the slice: x: 4, y: 8, z: 8 (z_hi: 2, z_lo: 4; z = z_hi * 4 + z_lo), core: 2. Of those that a mesh axis runs over, the one named last changes fastest.
Arguments:
- states: bfloat16 [128, 1024, 1024], P('layer', 'dp'), may hold values from -6 to 6
- weights: bfloat16 [128, 1024, 1024], P('layer', 'dp', 'mp'), may hold values from -0.1875 to 0.1875
- guess_points: bfloat16 [32, 1024, 1024], P('layer', 'dp'), may hold values from -2 to 2
- cotangent: bfloat16 [1024, 1024], P('dp'), may hold values from -6 to 6
Outputs:
- adjoint: bfloat16 [128, 1024, 1024], P('layer', 'dp', 'mp')
- weight_grads: float32 [128, 1024, 1024], P('layer', 'dp', 'mp')
All inputs are finite; a program needn't handle non-finite values.
Results may differ from a plain program's by a relative error of at most 0.03.
Values may be sent and summed in bfloat16 or wider, within the bound.
No kernel may reach another device: no remote copies, remote signals or barrier semaphores. Data moves between devices by JAX's collectives and lax.ppermute only.
A program may use at most 64 MiB of HBM per device.

v0:
```python
import jax
import jax.numpy as jnp
from jax import lax
from jax.sharding import PartitionSpec as P

step_size = 0.1


def from_behind(value, axis, steps):
    count = lax.axis_size(axis)
    leading, last = (max(0, -steps), min(count, count - steps))
    return lax.ppermute(value, axis, [(source, source + steps) for source in range(leading, last)])


def shortened(array):
    return jax.tree.map(lambda a: a.astype(jnp.bfloat16) if a.dtype == jnp.float32 else a, array)


def slope_of(inputs, weight_block):
    tangent = jnp.tanh(jnp.dot(inputs, weight_block, preferred_element_type=jnp.float32))
    return 1.0 - tangent * tangent


def back_product(scaled_rows, weight_block):
    return lax.dot_general(
        scaled_rows, weight_block, (((1,), (1,)), ((), ())), preferred_element_type=jnp.float32
    )


def body(states, weights, guess_points, cotangent):
    slab_count = lax.axis_size("layer")
    slab_index = lax.axis_index("layer")
    half_index = lax.axis_index("mp")
    layer_count, row_count, model_width = states.shape
    point_count = guess_points.shape[0]
    factor = layer_count // point_count
    columns = weights.shape[2]
    half_rows = row_count // lax.axis_size("mp")
    row_start = half_index * half_rows
    col_start = half_index * columns
    gathered = lax.all_gather(weights, "dp", axis=1, tiled=True)
    next_point = from_behind(guess_points[0], "layer", -1)
    terminal = jnp.where(
        slab_index == slab_count - 1, cotangent.astype(jnp.float32), next_point.astype(jnp.float32)
    )
    guess_wide = guess_points.astype(jnp.float32)
    slopes = [slope_of(states[layer_id], gathered[layer_id]) for layer_id in range(layer_count)]

    def scale_columns(upper_adj, layer_id):
        own_part = lax.dynamic_slice_in_dim(upper_adj, col_start, columns, 1)
        return (own_part * slopes[layer_id]).astype(jnp.bfloat16)

    def fine_step(upper_adj, scaled_rows, layer_id):
        summed = lax.psum(back_product(scaled_rows, gathered[layer_id]), "mp")
        return upper_adj + step_size * summed

    upper_adj = terminal
    residuals = [None] * point_count
    for layer_id in range(layer_count - 1, -1, -1):
        relaxed = fine_step(upper_adj, scale_columns(upper_adj, layer_id), layer_id)
        if layer_id % factor == 0:
            residuals[layer_id // factor] = relaxed - guess_wide[layer_id // factor]
            upper_adj = guess_wide[layer_id // factor]
        else:
            upper_adj = relaxed
    residual_half = lax.dynamic_slice_in_dim(jnp.stack(residuals), row_start, half_rows, 1)
    coarse_weights = lax.all_gather(gathered[::factor], "mp", axis=2, tiled=True)
    state_half = lax.dynamic_slice_in_dim(states[::factor], row_start, half_rows, 1)
    coarse_slopes = jnp.stack([slope_of(state_half[0], coarse_weights[0])])

    def coarse_solve(incoming):
        carried = incoming.astype(jnp.float32)
        results = [None] * point_count
        scaled_rows = (carried * coarse_slopes[0]).astype(jnp.bfloat16)
        stepped = (
            carried
            + factor * step_size * back_product(scaled_rows, coarse_weights[0])
            + residual_half[0]
        )
        results[0] = stepped.astype(jnp.bfloat16)
        return jnp.stack(results)

    def solve_pair(operand_pair):
        return coarse_solve(operand_pair[0])

    def keep_pair(operand_pair):
        return operand_pair[1]

    def one_turn(turn_id, loop_state):
        incoming, errors = loop_state
        errors = lax.cond(
            turn_id == slab_count - 1 - slab_index, solve_pair, keep_pair, (incoming, errors)
        )
        incoming = from_behind(shortened(errors[0]), "layer", -1)
        return (incoming, errors)

    start_in = jnp.zeros((half_rows, model_width), jnp.bfloat16)
    start_errors = jnp.zeros((point_count, half_rows, model_width), jnp.bfloat16)
    incoming, errors = lax.fori_loop(0, slab_count - 1, one_turn, (start_in, start_errors))
    errors = lax.cond(slab_index == 0, solve_pair, keep_pair, (incoming, errors))
    adjoint_parts = [None] * layer_count
    scaled_parts = [None] * layer_count
    spread = lax.all_gather(
        shortened(jnp.concatenate([errors, incoming[None]], 0)), "mp", axis=1, tiled=True
    )
    upper_adj = terminal + spread[point_count].astype(jnp.float32)
    for layer_id in range(layer_count - 1, -1, -1):
        scaled_rows = scale_columns(upper_adj, layer_id)
        if layer_id % factor == 0:
            current = guess_wide[layer_id // factor] + spread[layer_id // factor].astype(
                jnp.float32
            )
        else:
            current = fine_step(upper_adj, scaled_rows, layer_id)
        adjoint_parts[layer_id] = lax.dynamic_slice_in_dim(current, col_start, columns, 1).astype(
            jnp.bfloat16
        )
        scaled_parts[layer_id] = scaled_rows
        upper_adj = current
    adjoint_out = jnp.stack(adjoint_parts)
    scaled_out = jnp.stack(scaled_parts)
    partial_terms = jnp.einsum(
        "lrd,lrh->ldh", states, scaled_out, preferred_element_type=jnp.float32
    )
    weight_grads = step_size * lax.psum_scatter(
        partial_terms.astype(jnp.bfloat16), "dp", scatter_dimension=1, tiled=True
    ).astype(jnp.float32)
    return (adjoint_out, weight_grads)


def solution(mesh):
    return jax.shard_map(
        body,
        mesh=mesh,
        in_specs=(
            P("layer", "dp", None),
            P("layer", "dp", "mp"),
            P("layer", "dp", None),
            P("dp", None),
        ),
        out_specs=(P("layer", "dp", "mp"), P("layer", "dp", "mp")),
        check_vma=False,
    )
```

profile of v0, /device:TPU:1, one launch (start us, length us, event | category | flops | bytes accessed | tf_op | source)
XLA Modules:
  0.0 934.7 jit_solution(8836864910243469288)
XLA Ops:
  8.0 8.7 collective-permute-start.1
  19.1 53.4 %all-gather.3.cloned.1.call-done = bf16[4,1024,512]{2,1,0:T(8,128)(2,1)} async-done(((bf16[4,128,512]{2,1,0:T(8,128)(2,1)}), bf16[4,1024,512]{2,1,0:T(8,128)(2,1)}) %all-gather.3.cloned.1.call-update) | async-done | bytes 4194320 | tf_op jit(solution)/shard_map/all_gather | solution.py:41
  74.1 2.6 fusion.61
  78.4 59.1 %all-reduce.8.cloned.1.call-done = f32[128,1024]{1,0:T(8,128)} async-done(((f32[128,1024]{1,0:T(8,128)}), f32[128,1024]{1,0:T(8,128)}) %all-reduce.8.cloned.1.call-update) | async-done | bytes 524304 | tf_op jit(solution)/shard_map/psum | solution.py:54
  138.6 2.5 fusion.63
  142.7 56.4 %all-reduce.10.cloned.1.call-done = f32[128,1024]{1,0:T(8,128)} async-done(((f32[128,1024]{1,0:T(8,128)}), f32[128,1024]{1,0:T(8,128)}) %all-reduce.10.cloned.1.call-update) | async-done | bytes 524304 | tf_op jit(solution)/shard_map/psum | solution.py:54
  200.2 2.5 fusion.65
  202.8 2.3 slice.51
  205.2 2.3 fusion.56
  207.4 53.4 %all-reduce.12.cloned.1.call-done = f32[128,1024]{1,0:T(8,128)} async-done(((f32[128,1024]{1,0:T(8,128)}), f32[128,1024]{1,0:T(8,128)}) %all-reduce.12.cloned.1.call-update) | async-done | bytes 524304 | tf_op jit(solution)/shard_map/psum | solution.py:54
  261.9 2.6 fusion.57
  265.6 62.4 %all-gather.5.cloned.1.call-done = bf16[1,1024,1024]{2,1,0:T(8,128)(2,1)} async-done(((bf16[1,1024,512]{2,1,0:T(8,128)(2,1)}), bf16[1,1024,1024]{2,1,0:T(8,128)(2,1)}) %all-gather.5.cloned.1.call-update) | async-done | bytes 2097168 | tf_op jit(solution)/shard_map/all_gather | solution.py:67
  327.9 2.1 fusion.46
  330.0 59.3 %all-reduce.14.cloned.1.call-done = f32[128,1024]{1,0:T(8,128)} async-done(((f32[128,1024]{1,0:T(8,128)}), f32[128,1024]{1,0:T(8,128)}) %all-reduce.14.cloned.1.call-update) | async-done | bytes 524304 | tf_op jit(solution)/shard_map/psum | solution.py:54
  390.3 250.6 %while.23 = (s32[]{:T(128)}, bf16[64,1024]{1,0:T(8,128)(2,1)S(1)}, bf16[1,64,1024]{2,1,0:T(8,128)(2,1)S(1)}, s32[]{:T(128)}, f32[64,1024]{1,0:T(8,128)S(1)}, /*i...) while((s32[]{:T(128)}, bf16[64,1024]{1,0:T(8,128)(2,1)S(1)}, ...), condition=%wide.region_7.8_spmd, body=%wide.region_4.7_spmd.sunk | while | flops 134742016 | bytes 3408051 | solution.py:99
  390.4 2.7 collective-permute-start
  393.1 3.9 collective-permute-done
  397.0 1.9 collective-permute-start
  398.9 4.4 collective-permute-done
  405.2 4.4 collective-permute-done
  411.5 4.4 collective-permute-done
  417.7 4.4 collective-permute-done
  424.0 4.4 collective-permute-done
  430.3 4.4 collective-permute-done
  436.6 4.4 collective-permute-done
  442.8 4.4 collective-permute-done
  449.1 4.4 collective-permute-done
  455.4 4.4 collective-permute-done
  459.8 1.9 collective-permute-start
  461.7 5.5 collective-permute-done
  469.0 6.5 collective-permute-done
  477.4 6.5 collective-permute-done
  485.8 6.5 collective-permute-done
  494.2 6.5 collective-permute-done
  500.7 1.9 collective-permute-start
  502.6 6.5 collective-permute-done
  511.0 6.5 collective-permute-done
  519.4 6.5 collective-permute-done
  527.7 6.5 collective-permute-done
  536.1 6.5 collective-permute-done
  544.5 6.5 collective-permute-done
  552.9 6.5 collective-permute-done
  561.3 6.5 collective-permute-done
  569.7 6.5 collective-permute-done
  578.1 6.5 collective-permute-done
  586.5 6.5 collective-permute-done
  594.8 6.5 collective-permute-done
  603.2 6.5 collective-permute-done
  611.6 20.7 %collective-permute-done = bf16[64,1024]{1,0:T(8,128)(2,1)S(1)} collective-permute-done((bf16[64,1024]{1,0:T(8,128)(2,1)S(1)}, bf16[64,1024]{1,0:T(8,128)(2,1)S(1)}, u32[]{:S(2)}, u32[]{:S(2)}) %collective-permute-start) | collective-permute-done | bytes 131104 | tf_op jit(solution)/shard_map/while/body/eval_jaxpr/ppermute | solution.py:12
  632.3 2.4 conditional.4
  632.3 2.4 fusion.14
  634.6 1.9 collective-permute-start
  636.6 4.4 collective-permute-done
  641.0 15.2 %all_gather.11 = bf16[2,128,1024]{2,1,0:T(8,128)(2,1)S(1)} all-gather(bf16[2,64,1024]{2,1,0:T(8,128)(2,1)S(1)} %pad_maximum_fusion.1), channel_id=1, replica_groups=mesh['layer'=32,'dp'=8,'mp'=2] {'mp'}, dimensions={1}, use_global_device_ids=true | all-gather | bytes 786432 | tf_op jit(solution)/shard_map/all_gather | solution.py:103
  656.3 2.5 fusion.60
  658.9 69.1 %all-reduce.16.cloned.1.call-done = f32[128,1024]{1,0:T(8,128)} async-done(((f32[128,1024]{1,0:T(8,128)}), f32[128,1024]{1,0:T(8,128)}) %all-reduce.16.cloned.1.call-update) | async-done | bytes 524304 | tf_op jit(solution)/shard_map/psum | solution.py:54
  729.2 2.5 fusion.62
  731.7 58.0 %all-reduce.18.cloned.1.call-done = f32[128,1024]{1,0:T(8,128)} async-done(((f32[128,1024]{1,0:T(8,128)}), f32[128,1024]{1,0:T(8,128)}) %all-reduce.18.cloned.1.call-update) | async-done | bytes 524304 | tf_op jit(solution)/shard_map/psum | solution.py:54
  790.9 2.5 fusion.64
  793.4 58.0 %all-reduce.20.cloned.1.call-done = f32[128,1024]{1,0:T(8,128)} async-done(((f32[128,1024]{1,0:T(8,128)}), f32[128,1024]{1,0:T(8,128)}) %all-reduce.20.cloned.1.call-update) | async-done | bytes 524304 | tf_op jit(solution)/shard_map/psum | solution.py:54
  852.4 4.5 convert_bitcast_fusion
  856.9 7.8 copy.11
  864.7 5.6 copy.13
  871.3 53.3 %reduce-scatter.4.cloned.1.call-done = bf16[128,2048]{1,0:T(8,128)(2,1)} async-done(((bf16[1024,2048]{1,0:T(8,128)(2,1)}), bf16[128,2048]{1,0:T(8,128)(2,1)}) %reduce-scatter.4.cloned.1.call-update) | async-done | bytes 524304
  (116 shorter events, 70.9 us)
Async XLA Ops:
  7.2 69.6 %copy-start = (bf16[4,128,1024]{2,1,0:T(8,128)(2,1)S(1)}, bf16[4,128,1024]{2,1,0:T(8,128)(2,1)}, u32[]{:S(2)}) copy-start(bf16[4,128,1024]{2,1,0:T(8,128)(2,1)} %param.10) | copy-start | bytes 3145732
  7.2 65.3 %all-gather.3.cloned.1.call-start = ((), (), s32[]{:S(2)}) async-start(), calls=%async_computation.1 | async-start | bytes 4718592 | tf_op jit(solution)/shard_map/all_gather | solution.py:41
  7.9 129.6 %all-reduce.8.cloned.1.call-start = ((), (), s32[]{:S(2)}) async-start(), calls=%async_computation.3 | async-start | bytes 1048576 | tf_op jit(solution)/shard_map/psum | solution.py:54
  8.0 10.1 %collective-permute-start.1 = (bf16[128,1024]{1,0:T(8,128)(2,1)}, bf16[128,1024]{1,0:T(8,128)(2,1)S(1)}, u32[]{:S(2)}, u32[]{:S(2)}) collective-permute-start(bf16[128,1024]{1,0:T(8,128)(2,1)} %bitcast.126), channel_id=1, source_target_pairs={{16,0},{32,16},{48,32},{64,48},{80,64},{96,80},{112,96},{128,112},... | collective-permute-start | bytes 786440 | tf_op jit(solution)/shard_map/ppermute | solution.py:12
  74.1 4.2 copy-start.1
  76.8 122.4 %all-reduce.10.cloned.1.call-start = ((), (), s32[]{:S(2)}) async-start(), calls=%async_computation.4 | async-start | bytes 1048576 | tf_op jit(solution)/shard_map/psum | solution.py:54
  141.1 119.7 %all-reduce.12.cloned.1.call-start = ((), (), s32[]{:S(2)}) async-start(), calls=%async_computation.5 | async-start | bytes 1048576 | tf_op jit(solution)/shard_map/psum | solution.py:54
  202.8 125.2 %all-gather.5.cloned.1.call-start = ((), (), s32[]{:S(2)}) async-start(), calls=%async_computation.2 | async-start | bytes 3145728 | tf_op jit(solution)/shard_map/all_gather | solution.py:67
  205.1 122.9 %slice-start = ((bf16[4,128,1024]{2,1,0:T(8,128)(2,1)}), bf16[1,128,1024]{2,1,0:T(8,128)(2,1)S(1)}, s32[]{:S(2)}) async-start(bf16[4,128,1024]{2,1,0:T(8,128)(2,1)} %param.10), calls=%async_computation.11 | async-start | bytes 524288 | tf_op jit(solution)/shard_map/slice | solution.py:68
  205.1 184.2 %all-reduce.14.cloned.1.call-start = ((), (), s32[]{:S(2)}) async-start(), calls=%async_computation.6 | async-start | bytes 1048576 | tf_op jit(solution)/shard_map/psum | solution.py:54
  264.5 463.5 %all-reduce.16.cloned.1.call-start = ((), (), s32[]{:S(2)}) async-start(), calls=%async_computation.7 | async-start | bytes 1048576 | tf_op jit(solution)/shard_map/psum | solution.py:54
  390.4 6.6 collective-permute-start
  397.0 6.3 collective-permute-start
  403.3 6.3 collective-permute-start
  409.5 6.3 collective-permute-start
  415.8 6.3 collective-permute-start
  422.1 6.3 collective-permute-start
  428.4 6.3 collective-permute-start
  434.6 6.3 collective-permute-start
  440.9 6.3 collective-permute-start
  447.2 6.3 collective-permute-start
  453.5 6.3 collective-permute-start
  459.8 7.4 collective-permute-start
  467.1 8.4 collective-permute-start
  475.5 8.4 collective-permute-start
  483.9 8.4 collective-permute-start
  492.3 8.4 collective-permute-start
  500.7 8.4 collective-permute-start
  509.1 8.4 collective-permute-start
  517.4 8.4 collective-permute-start
  525.8 8.4 collective-permute-start
  534.2 8.4 collective-permute-start
  542.6 8.4 collective-permute-start
  551.0 8.4 collective-permute-start
  559.4 8.4 collective-permute-start
  567.8 8.4 collective-permute-start
  576.1 8.4 collective-permute-start
  584.5 8.4 collective-permute-start
  592.9 8.4 collective-permute-start
  601.3 8.4 collective-permute-start
  609.7 22.6 %collective-permute-start = (bf16[64,1024]{1,0:T(8,128)(2,1)S(1)}, bf16[64,1024]{1,0:T(8,128)(2,1)S(1)}, u32[]{:S(2)}, u32[]{:S(2)}) collective-permute-start(bf16[64,1024]{1,0:T(8,128)(2,1)S(1)} %bitcast.125), channel_id=1, source_target_pairs={{16,0},{32,16},{48,32},{64,48},{80,64},{96,80},{112,96},{128,112},... | collective-permute-start | bytes 393224 | tf_op jit(solution)/shard_map/while/body/eval_jaxpr/ppermute | solution.py:12
  634.6 6.3 collective-permute-start
  640.9 15.3 %copy-start.2 = (f32[128,512]{1,0:T(8,128)S(1)}, f32[128,512]{1,0:T(8,128)}, u32[]{:S(2)}) copy-start(f32[128,512]{1,0:T(8,128)} %copy-done.1) | copy-start | bytes 786436
  658.8 192.6 %copy-start.3 = (f32[128,512]{1,0:T(8,128)S(1)}, f32[128,512]{1,0:T(8,128)}, u32[]{:S(2)}) copy-start(f32[128,512]{1,0:T(8,128)} %fusion.56) | copy-start | bytes 786436
  658.9 130.8 %all-reduce.18.cloned.1.call-start = ((), (), s32[]{:S(2)}) async-start(), calls=%async_computation.8 | async-start | bytes 1048576 | tf_op jit(solution)/shard_map/psum | solution.py:54
  731.7 119.7 %all-reduce.20.cloned.1.call-start = ((), (), s32[]{:S(2)}) async-start(), calls=%async_computation.9 | async-start | bytes 1048576 | tf_op jit(solution)/shard_map/psum | solution.py:54
  793.4 131.2 %reduce-scatter.4.cloned.1.call-start = ((), (), s32[]{:S(2)}) async-start(), calls=%async_computation.10 | async-start | bytes 4718592
Sparse Core Ops, SparseCore 0:
  10.1 62.3 all-gather.2
  76.9 60.5 all-reduce.7
  141.2 57.8 all-reduce.9
  202.9 57.8 all-reduce.11
  263.3 64.5 all-gather.4
  331.3 57.9 all-reduce.13
  659.0 68.9 all-reduce.15
  731.8 57.8 all-reduce.17
  793.5 57.8 all-reduce.19
  870.4 54.0 reduce-scatter.3
where the time goes:
time: 937 us; the launch traced here: 935 us
  waiting for transfers between devices  772 us (82%)
  starting transfers between devices  69.2 us (7%)
  matrix products  33.6 us (4%)
  local copies, waits for them, and re-layouts  18.9 us (2%)
  blocking collectives  15.2 us (2%)
  between operations  14.4 us (2%)
  other arithmetic  10.7 us (1%)
    psum x7, waiting for transfers between devices, fine_step(): summed = lax.psum(back_product(scaled_rows, gathered[layer_id]), 'mp')  413 us
    ppermute x32, waiting for transfers between devices, from_behind(): lax.ppermute(value, axis, [(source, source + steps) for source in range(l...  189 us
    ppermute x32, starting transfers between devices, from_behind(): lax.ppermute(value, axis, [(source, source + steps) for source in range(l...  68.8 us
    all_gather x1, waiting for transfers between devices, body(): lax.all_gather(gathered[::factor], 'mp', axis=2, tiled=True)  62.4 us
    unnamed x11, waiting for transfers between devices  54.1 us
    all_gather x1, waiting for transfers between devices, body(): gathered = lax.all_gather(weights, 'dp', axis=1, tiled=True)  53.4 us
    dot_general x8, matrix products, back_product(): lax.dot_general(scaled_rows, weight_block, (((1,), (1,)), ((), ())), pref...  20 us
  transfers between devices with their start and end apart: 42, of which 42 were waited for; matrix products, arithmetic and copies ran while one was open for 2% of the time, Pallas kernels for 0%

commit v1 on v0

--- a/solution.py
+++ b/solution.py
@@ -2,6 +2,7 @@
 import jax.numpy as jnp
 from jax import lax
 from jax.sharding import PartitionSpec as P
+from jax.lax import all_gather
 
 step_size = 0.1
 
@@ -51,7 +52,8 @@
         return (own_part * slopes[layer_id]).astype(jnp.bfloat16)
 
     def fine_step(upper_adj, scaled_rows, layer_id):
-        summed = lax.psum(back_product(scaled_rows, gathered[layer_id]), "mp")
+        _fix_run = lambda arr: jnp.sum(all_gather(arr, "mp"), axis=0)
+        summed = _fix_run(back_product(scaled_rows, gathered[layer_id]))
         return upper_adj + step_size * summed
 
     upper_adj = terminal

time: 937 us -> 833 us (0.89)
  waiting for transfers between devices: 772 us -> 663 us
    psum x7 -> x0, waiting for transfers between devices: 413 us -> none  [fine_step(): summed = lax.psum(back_product(scaled_rows, gathered[layer_id]), 'mp')]
    all_gather x0 -> x7, waiting for transfers between devices: none -> 306 us  [fine_step(): _fix_run = lambda arr: jnp.sum(all_gather(arr, 'mp'), axis=0)]
    reduce_sum x0 -> x7, other arithmetic: none -> 10.3 us  [fine_step(): _fix_run = lambda arr: jnp.sum(all_gather(arr, 'mp'), axis=0)]
where the time goes in v1:
time: 833 us; the launch traced here: 831 us
  waiting for transfers between devices  663 us (80%)
  starting transfers between devices  69.2 us (8%)
  matrix products  31.8 us (4%)
  local copies, waits for them, and re-layouts  21.3 us (3%)
  other arithmetic  19.3 us (2%)
  between operations  14.5 us (2%)
  blocking collectives  11.6 us (1%)
    all_gather x7, waiting for transfers between devices, fine_step(): _fix_run = lambda arr: jnp.sum(all_gather(arr, 'mp'), axis=0)  306 us
    ppermute x32, waiting for transfers between devices, from_behind(): lax.ppermute(value, axis, [(source, source + steps) for source in range(l...  190 us
    ppermute x32, starting transfers between devices, from_behind(): lax.ppermute(value, axis, [(source, source + steps) for source in range(l...  68.8 us
    all_gather x1, waiting for transfers between devices, body(): lax.all_gather(gathered[::factor], 'mp', axis=2, tiled=True)  60.9 us
    all_gather x1, waiting for transfers between devices, body(): gathered = lax.all_gather(weights, 'dp', axis=1, tiled=True)  53.4 us
    unnamed x11, waiting for transfers between devices  53 us
    dot_general x8, matrix products, back_product(): lax.dot_general(scaled_rows, weight_block, (((1,), (1,)), ((), ())), pref...  19.2 us
    unnamed x28, local copies, waits for them, and re-layouts  18.3 us
  transfers between devices with their start and end apart: 42, of which 42 were waited for; matrix products, arithmetic and copies ran while one was open for 2% of the time, Pallas kernels for 0%

profile of v1, /device:TPU:1, one launch (start us, length us, event | category | flops | bytes accessed | tf_op | source)
XLA Modules:
  0.0 830.8 jit_solution(10649964009465406608)
XLA Ops:
  8.0 8.7 %collective-permute-start.1 = (bf16[128,1024]{1,0:T(8,128)(2,1)}, bf16[128,1024]{1,0:T(8,128)(2,1)S(1)}, u32[]{:S(2)}, u32[]{:S(2)}) collective-permute-start(bf16[128,1024]{1,0:T(8,128)(2,1)} %bitcast.139), channel_id=1, source_target_pairs={{16,0},{32,16},{48,32},{64,48},{80,64},{96,80},{112,96},{128,112},... | collective-permute-start | bytes 786440 | tf_op jit(solution)/shard_map/ppermute | solution.py:13
  19.1 53.4 %all-gather.17.cloned.1.call-done = bf16[4,1024,512]{2,1,0:T(8,128)(2,1)} async-done(((bf16[4,128,512]{2,1,0:T(8,128)(2,1)}), bf16[4,1024,512]{2,1,0:T(8,128)(2,1)}) %all-gather.17.cloned.1.call-update) | async-done | bytes 4194320 | tf_op jit(solution)/shard_map/all_gather | solution.py:42
  74.8 2.5 fusion.61
  79.0 42.6 %all-gather.21.cloned.1.call-done = f32[256,1024]{1,0:T(8,128)} async-done(((f32[128,1024]{1,0:T(8,128)}), f32[256,1024]{1,0:T(8,128)}) %all-gather.21.cloned.1.call-update) | async-done | bytes 1048592 | tf_op jit(solution)/shard_map/all_gather | solution.py:55
  123.0 2.5 fusion.63
  127.2 39.9 %all-gather.23.cloned.1.call-done = f32[256,1024]{1,0:T(8,128)} async-done(((f32[128,1024]{1,0:T(8,128)}), f32[256,1024]{1,0:T(8,128)}) %all-gather.23.cloned.1.call-update) | async-done | bytes 1048592 | tf_op jit(solution)/shard_map/all_gather | solution.py:55
  168.4 2.5 fusion.65
  171.0 2.3 slice.51
  173.4 2.3 fusion.56
  175.7 36.8 %all-gather.25.cloned.1.call-done = f32[256,1024]{1,0:T(8,128)} async-done(((f32[128,1024]{1,0:T(8,128)}), f32[256,1024]{1,0:T(8,128)}) %all-gather.25.cloned.1.call-update) | async-done | bytes 1048592 | tf_op jit(solution)/shard_map/all_gather | solution.py:55
  213.9 2.8 fusion.57
  218.6 60.9 %all-gather.19.cloned.1.call-done = bf16[1,1024,1024]{2,1,0:T(8,128)(2,1)} async-done(((bf16[1,1024,512]{2,1,0:T(8,128)(2,1)}), bf16[1,1024,1024]{2,1,0:T(8,128)(2,1)}) %all-gather.19.cloned.1.call-update) | async-done | bytes 2097168 | tf_op jit(solution)/shard_map/all_gather | solution.py:69
  279.5 2.2 fusion.46
  281.7 41.3 %all-gather.27.cloned.1.call-done = f32[256,1024]{1,0:T(8,128)} async-done(((f32[128,1024]{1,0:T(8,128)}), f32[256,1024]{1,0:T(8,128)}) %all-gather.27.cloned.1.call-update) | async-done | bytes 1048592 | tf_op jit(solution)/shard_map/all_gather | solution.py:55
  323.0 2.1 reduce_sum.66
  327.0 250.4 %while.23 = (s32[]{:T(128)}, bf16[64,1024]{1,0:T(8,128)(2,1)S(1)}, bf16[1,64,1024]{2,1,0:T(8,128)(2,1)}, s32[]{:T(128)}, f32[64,1024]{1,0:T(8,128)S(1)}, /*index...) while((s32[]{:T(128)}, bf16[64,1024]{1,0:T(8,128)(2,1)S(1)}, ...), condition=%wide.region_7.8_spmd, body=%wide.region_4.7_spmd.sunk | while | flops 134742016 | bytes 3408051 | solution.py:101
  327.0 2.8 collective-permute-start
  329.8 3.9 collective-permute-done
  333.7 1.9 collective-permute-start
  335.6 4.6 collective-permute-done
  340.2 1.9 collective-permute-start
  342.1 4.6 collective-permute-done
  346.7 1.9 collective-permute-start
  348.6 4.6 collective-permute-done
  353.2 1.9 collective-permute-start
  355.1 4.6 collective-permute-done
  361.6 4.6 collective-permute-done
  368.1 4.6 collective-permute-done
  374.6 4.6 collective-permute-done
  381.0 4.6 collective-permute-done
  387.5 4.6 collective-permute-done
  394.0 4.6 collective-permute-done
  400.5 5.7 collective-permute-done
  408.1 6.7 collective-permute-done
  416.7 6.7 collective-permute-done
  425.3 6.7 collective-permute-done
  433.9 6.7 collective-permute-done
  442.5 6.7 collective-permute-done
  451.1 6.7 collective-permute-done
  459.7 6.7 collective-permute-done
  468.3 6.7 collective-permute-done
  476.9 6.7 collective-permute-done
  485.5 6.7 collective-permute-done
  494.1 6.7 collective-permute-done
  502.6 6.7 collective-permute-done
  511.2 6.7 collective-permute-done
  517.9 1.9 collective-permute-start
  519.8 6.7 collective-permute-done
  528.4 6.7 collective-permute-done
  537.0 6.7 collective-permute-done
  545.6 6.7 collective-permute-done
  554.2 15.2 %collective-permute-done = bf16[64,1024]{1,0:T(8,128)(2,1)S(1)} collective-permute-done((bf16[64,1024]{1,0:T(8,128)(2,1)}, bf16[64,1024]{1,0:T(8,128)(2,1)S(1)}, u32[]{:S(2)}, u32[]{:S(2)}) %collective-permute-start) | collective-permute-done | bytes 131104 | tf_op jit(solution)/shard_map/while/body/eval_jaxpr/ppermute | solution.py:13
  572.8 4.6 collective-permute-done
  578.4 11.6 %all_gather.61 = bf16[2,128,1024]{2,1,0:T(8,128)(2,1)S(1)} all-gather(bf16[2,64,1024]{2,1,0:T(8,128)(2,1)S(1)} %pad_maximum_fusion.1), channel_id=1, replica_groups=mesh['layer'=32,'dp'=8,'mp'=2] {'mp'}, dimensions={1}, use_global_device_ids=true | all-gather | bytes 786432 | tf_op jit(solution)/shard_map/all_gather | solution.py:105
  590.0 2.5 fusion.60
  592.6 62.2 %all-gather.29.cloned.1.call-done = f32[256,1024]{1,0:T(8,128)} async-done(((f32[128,1024]{1,0:T(8,128)}), f32[256,1024]{1,0:T(8,128)}) %all-gather.29.cloned.1.call-update) | async-done | bytes 1048592 | tf_op jit(solution)/shard_map/all_gather | solution.py:55
  656.2 2.5 fusion.62
  658.8 41.4 %all-gather.31.cloned.1.call-done = f32[256,1024]{1,0:T(8,128)} async-done(((f32[128,1024]{1,0:T(8,128)}), f32[256,1024]{1,0:T(8,128)}) %all-gather.31.cloned.1.call-update) | async-done | bytes 1048592 | tf_op jit(solution)/shard_map/all_gather | solution.py:55
  702.7 2.5 fusion.64
  705.3 41.4 %all-gather.33.cloned.1.call-done = f32[256,1024]{1,0:T(8,128)} async-done(((f32[128,1024]{1,0:T(8,128)}), f32[256,1024]{1,0:T(8,128)}) %all-gather.33.cloned.1.call-update) | async-done | bytes 1048592 | tf_op jit(solution)/shard_map/all_gather | solution.py:55
  749.8 3.3 convert_bitcast_fusion
  753.1 7.8 copy.11
  760.9 5.6 copy.13
  768.6 52.1 %reduce-scatter.4.cloned.1.call-done = bf16[128,2048]{1,0:T(8,128)(2,1)} async-done(((bf16[1024,2048]{1,0:T(8,128)(2,1)}), bf16[128,2048]{1,0:T(8,128)(2,1)}) %reduce-scatter.4.cloned.1.call-update) | async-done | bytes 524304
  (137 shorter events, 80.7 us)
Async XLA Ops:
  7.2 70.2 %copy-start.3 = (bf16[4,128,1024]{2,1,0:T(8,128)(2,1)S(1)}, bf16[4,128,1024]{2,1,0:T(8,128)(2,1)}, u32[]{:S(2)}) copy-start(bf16[4,128,1024]{2,1,0:T(8,128)(2,1)} %param.10) | copy-start | bytes 3145732
  7.2 65.3 %all-gather.17.cloned.1.call-start = ((), (), s32[]{:S(2)}) async-start(), calls=%async_computation.1 | async-start | bytes 4718592 | tf_op jit(solution)/shard_map/all_gather | solution.py:42
  7.9 113.7 %all-gather.21.cloned.1.call-start = ((), (), s32[]{:S(2)}) async-start(), calls=%async_computation.3 | async-start | bytes 1572864 | tf_op jit(solution)/shard_map/all_gather | solution.py:55
  8.0 10.1 %collective-permute-start.1 = (bf16[128,1024]{1,0:T(8,128)(2,1)}, bf16[128,1024]{1,0:T(8,128)(2,1)S(1)}, u32[]{:S(2)}, u32[]{:S(2)}) collective-permute-start(bf16[128,1024]{1,0:T(8,128)(2,1)} %bitcast.139), channel_id=1, source_target_pairs={{16,0},{32,16},{48,32},{64,48},{80,64},{96,80},{112,96},{128,112},... | collective-permute-start | bytes 786440 | tf_op jit(solution)/shard_map/ppermute | solution.py:13
  74.1 0.7 copy-start.8
  77.3 89.7 %all-gather.23.cloned.1.call-start = ((), (), s32[]{:S(2)}) async-start(), calls=%async_computation.4 | async-start | bytes 1572864 | tf_op jit(solution)/shard_map/all_gather | solution.py:55
  79.0 88.1 %copy-start.6 = (f32[128,512]{1,0:T(8,128)}, f32[128,512]{1,0:T(8,128)S(1)}, u32[]{:S(2)}) copy-start(f32[128,512]{1,0:T(8,128)S(1)} %fusion.54) | copy-start | bytes 786436
  125.5 86.9 %all-gather.25.cloned.1.call-start = ((), (), s32[]{:S(2)}) async-start(), calls=%async_computation.5 | async-start | bytes 1572864 | tf_op jit(solution)/shard_map/all_gather | solution.py:55
  127.1 46.1 %copy-start.5 = (f32[128,512]{1,0:T(8,128)}, f32[128,512]{1,0:T(8,128)S(1)}, u32[]{:S(2)}) copy-start(f32[128,512]{1,0:T(8,128)S(1)} %fusion.55) | copy-start | bytes 786436
  171.0 108.5 %all-gather.19.cloned.1.call-start = ((), (), s32[]{:S(2)}) async-start(), calls=%async_computation.2 | async-start | bytes 3145728 | tf_op jit(solution)/shard_map/all_gather | solution.py:69
  173.3 106.2 %slice-start = ((bf16[4,128,1024]{2,1,0:T(8,128)(2,1)}), bf16[1,128,1024]{2,1,0:T(8,128)(2,1)S(1)}, s32[]{:S(2)}) async-start(bf16[4,128,1024]{2,1,0:T(8,128)(2,1)} %param.10), calls=%async_computation.11 | async-start | bytes 524288 | tf_op jit(solution)/shard_map/slice | solution.py:70
  173.3 149.7 %all-gather.27.cloned.1.call-start = ((), (), s32[]{:S(2)}) async-start(), calls=%async_computation.6 | async-start | bytes 1572864 | tf_op jit(solution)/shard_map/all_gather | solution.py:55
  213.9 4.7 copy-start.1
  216.7 438.0 %all-gather.29.cloned.1.call-start = ((), (), s32[]{:S(2)}) async-start(), calls=%async_computation.7 | async-start | bytes 1572864 | tf_op jit(solution)/shard_map/all_gather | solution.py:55
  279.5 47.5 %copy-start = (bf16[1,1024,1024]{2,1,0:T(8,128)(2,1)S(1)}, bf16[1,1024,1024]{2,1,0:T(8,128)(2,1)}, u32[]{:S(2)}) copy-start(bf16[1,1024,1024]{2,1,0:T(8,128)(2,1)} %all-gather.19.cloned.1.call-done) | copy-start | bytes 6291460
  327.0 6.7 collective-permute-start
  333.7 6.5 collective-permute-start
  340.2 6.5 collective-permute-start
  346.7 6.5 collective-permute-start
  353.2 6.5 collective-permute-start
  359.7 6.5 collective-permute-start
  366.2 6.5 collective-permute-start
  372.6 6.5 collective-permute-start
  379.1 6.5 collective-permute-start
  385.6 6.5 collective-permute-start
  392.1 6.5 collective-permute-start
  398.6 7.6 collective-permute-start
  406.2 8.6 %collective-permute-start = (bf16[64,1024]{1,0:T(8,128)(2,1)}, bf16[64,1024]{1,0:T(8,128)(2,1)S(1)}, u32[]{:S(2)}, u32[]{:S(2)}) collective-permute-start(bf16[64,1024]{1,0:T(8,128)(2,1)} %bitcast.124), channel_id=1, source_target_pairs={{16,0},{32,16},{48,32},{64,48},{80,64},{96,80},{112,96},{128,112},... | collective-permute-start | bytes 393224 | tf_op jit(solution)/shard_map/while/body/eval_jaxpr/ppermute | solution.py:13
  414.8 8.6 %collective-permute-start = (bf16[64,1024]{1,0:T(8,128)(2,1)}, bf16[64,1024]{1,0:T(8,128)(2,1)S(1)}, u32[]{:S(2)}, u32[]{:S(2)}) collective-permute-start(bf16[64,1024]{1,0:T(8,128)(2,1)} %bitcast.124), channel_id=1, source_target_pairs={{16,0},{32,16},{48,32},{64,48},{80,64},{96,80},{112,96},{128,112},... | collective-permute-start | bytes 393224 | tf_op jit(solution)/shard_map/while/body/eval_jaxpr/ppermute | solution.py:13
  423.4 8.6 %collective-permute-start = (bf16[64,1024]{1,0:T(8,128)(2,1)}, bf16[64,1024]{1,0:T(8,128)(2,1)S(1)}, u32[]{:S(2)}, u32[]{:S(2)}) collective-permute-start(bf16[64,1024]{1,0:T(8,128)(2,1)} %bitcast.124), channel_id=1, source_target_pairs={{16,0},{32,16},{48,32},{64,48},{80,64},{96,80},{112,96},{128,112},... | collective-permute-start | bytes 393224 | tf_op jit(solution)/shard_map/while/body/eval_jaxpr/ppermute | solution.py:13
  432.0 8.6 %collective-permute-start = (bf16[64,1024]{1,0:T(8,128)(2,1)}, bf16[64,1024]{1,0:T(8,128)(2,1)S(1)}, u32[]{:S(2)}, u32[]{:S(2)}) collective-permute-start(bf16[64,1024]{1,0:T(8,128)(2,1)} %bitcast.124), channel_id=1, source_target_pairs={{16,0},{32,16},{48,32},{64,48},{80,64},{96,80},{112,96},{128,112},... | collective-permute-start | bytes 393224 | tf_op jit(solution)/shard_map/while/body/eval_jaxpr/ppermute | solution.py:13
  440.6 8.6 %collective-permute-start = (bf16[64,1024]{1,0:T(8,128)(2,1)}, bf16[64,1024]{1,0:T(8,128)(2,1)S(1)}, u32[]{:S(2)}, u32[]{:S(2)}) collective-permute-start(bf16[64,1024]{1,0:T(8,128)(2,1)} %bitcast.124), channel_id=1, source_target_pairs={{16,0},{32,16},{48,32},{64,48},{80,64},{96,80},{112,96},{128,112},... | collective-permute-start | bytes 393224 | tf_op jit(solution)/shard_map/while/body/eval_jaxpr/ppermute | solution.py:13
  449.2 8.6 %collective-permute-start = (bf16[64,1024]{1,0:T(8,128)(2,1)}, bf16[64,1024]{1,0:T(8,128)(2,1)S(1)}, u32[]{:S(2)}, u32[]{:S(2)}) collective-permute-start(bf16[64,1024]{1,0:T(8,128)(2,1)} %bitcast.124), channel_id=1, source_target_pairs={{16,0},{32,16},{48,32},{64,48},{80,64},{96,80},{112,96},{128,112},... | collective-permute-start | bytes 393224 | tf_op jit(solution)/shard_map/while/body/eval_jaxpr/ppermute | solution.py:13
  457.7 8.6 %collective-permute-start = (bf16[64,1024]{1,0:T(8,128)(2,1)}, bf16[64,1024]{1,0:T(8,128)(2,1)S(1)}, u32[]{:S(2)}, u32[]{:S(2)}) collective-permute-start(bf16[64,1024]{1,0:T(8,128)(2,1)} %bitcast.124), channel_id=1, source_target_pairs={{16,0},{32,16},{48,32},{64,48},{80,64},{96,80},{112,96},{128,112},... | collective-permute-start | bytes 393224 | tf_op jit(solution)/shard_map/while/body/eval_jaxpr/ppermute | solution.py:13
  466.3 8.6 %collective-permute-start = (bf16[64,1024]{1,0:T(8,128)(2,1)}, bf16[64,1024]{1,0:T(8,128)(2,1)S(1)}, u32[]{:S(2)}, u32[]{:S(2)}) collective-permute-start(bf16[64,1024]{1,0:T(8,128)(2,1)} %bitcast.124), channel_id=1, source_target_pairs={{16,0},{32,16},{48,32},{64,48},{80,64},{96,80},{112,96},{128,112},... | collective-permute-start | bytes 393224 | tf_op jit(solution)/shard_map/while/body/eval_jaxpr/ppermute | solution.py:13
  474.9 8.6 %collective-permute-start = (bf16[64,1024]{1,0:T(8,128)(2,1)}, bf16[64,1024]{1,0:T(8,128)(2,1)S(1)}, u32[]{:S(2)}, u32[]{:S(2)}) collective-permute-start(bf16[64,1024]{1,0:T(8,128)(2,1)} %bitcast.124), channel_id=1, source_target_pairs={{16,0},{32,16},{48,32},{64,48},{80,64},{96,80},{112,96},{128,112},... | collective-permute-start | bytes 393224 | tf_op jit(solution)/shard_map/while/body/eval_jaxpr/ppermute | solution.py:13
  483.5 8.6 %collective-permute-start = (bf16[64,1024]{1,0:T(8,128)(2,1)}, bf16[64,1024]{1,0:T(8,128)(2,1)S(1)}, u32[]{:S(2)}, u32[]{:S(2)}) collective-permute-start(bf16[64,1024]{1,0:T(8,128)(2,1)} %bitcast.124), channel_id=1, source_target_pairs={{16,0},{32,16},{48,32},{64,48},{80,64},{96,80},{112,96},{128,112},... | collective-permute-start | bytes 393224 | tf_op jit(solution)/shard_map/while/body/eval_jaxpr/ppermute | solution.py:13
  492.1 8.6 %collective-permute-start = (bf16[64,1024]{1,0:T(8,128)(2,1)}, bf16[64,1024]{1,0:T(8,128)(2,1)S(1)}, u32[]{:S(2)}, u32[]{:S(2)}) collective-permute-start(bf16[64,1024]{1,0:T(8,128)(2,1)} %bitcast.124), channel_id=1, source_target_pairs={{16,0},{32,16},{48,32},{64,48},{80,64},{96,80},{112,96},{128,112},... | collective-permute-start | bytes 393224 | tf_op jit(solution)/shard_map/while/body/eval_jaxpr/ppermute | solution.py:13
  500.7 8.6 %collective-permute-start = (bf16[64,1024]{1,0:T(8,128)(2,1)}, bf16[64,1024]{1,0:T(8,128)(2,1)S(1)}, u32[]{:S(2)}, u32[]{:S(2)}) collective-permute-start(bf16[64,1024]{1,0:T(8,128)(2,1)} %bitcast.124), channel_id=1, source_target_pairs={{16,0},{32,16},{48,32},{64,48},{80,64},{96,80},{112,96},{128,112},... | collective-permute-start | bytes 393224 | tf_op jit(solution)/shard_map/while/body/eval_jaxpr/ppermute | solution.py:13
  509.3 8.6 %collective-permute-start = (bf16[64,1024]{1,0:T(8,128)(2,1)}, bf16[64,1024]{1,0:T(8,128)(2,1)S(1)}, u32[]{:S(2)}, u32[]{:S(2)}) collective-permute-start(bf16[64,1024]{1,0:T(8,128)(2,1)} %bitcast.124), channel_id=1, source_target_pairs={{16,0},{32,16},{48,32},{64,48},{80,64},{96,80},{112,96},{128,112},... | collective-permute-start | bytes 393224 | tf_op jit(solution)/shard_map/while/body/eval_jaxpr/ppermute | solution.py:13
  517.9 8.6 %collective-permute-start = (bf16[64,1024]{1,0:T(8,128)(2,1)}, bf16[64,1024]{1,0:T(8,128)(2,1)S(1)}, u32[]{:S(2)}, u32[]{:S(2)}) collective-permute-start(bf16[64,1024]{1,0:T(8,128)(2,1)} %bitcast.124), channel_id=1, source_target_pairs={{16,0},{32,16},{48,32},{64,48},{80,64},{96,80},{112,96},{128,112},... | collective-permute-start | bytes 393224 | tf_op jit(solution)/shard_map/while/body/eval_jaxpr/ppermute | solution.py:13
  526.5 8.6 %collective-permute-start = (bf16[64,1024]{1,0:T(8,128)(2,1)}, bf16[64,1024]{1,0:T(8,128)(2,1)S(1)}, u32[]{:S(2)}, u32[]{:S(2)}) collective-permute-start(bf16[64,1024]{1,0:T(8,128)(2,1)} %bitcast.124), channel_id=1, source_target_pairs={{16,0},{32,16},{48,32},{64,48},{80,64},{96,80},{112,96},{128,112},... | collective-permute-start | bytes 393224 | tf_op jit(solution)/shard_map/while/body/eval_jaxpr/ppermute | solution.py:13
  535.1 8.6 %collective-permute-start = (bf16[64,1024]{1,0:T(8,128)(2,1)}, bf16[64,1024]{1,0:T(8,128)(2,1)S(1)}, u32[]{:S(2)}, u32[]{:S(2)}) collective-permute-start(bf16[64,1024]{1,0:T(8,128)(2,1)} %bitcast.124), channel_id=1, source_target_pairs={{16,0},{32,16},{48,32},{64,48},{80,64},{96,80},{112,96},{128,112},... | collective-permute-start | bytes 393224 | tf_op jit(solution)/shard_map/while/body/eval_jaxpr/ppermute | solution.py:13
  543.7 8.6 %collective-permute-start = (bf16[64,1024]{1,0:T(8,128)(2,1)}, bf16[64,1024]{1,0:T(8,128)(2,1)S(1)}, u32[]{:S(2)}, u32[]{:S(2)}) collective-permute-start(bf16[64,1024]{1,0:T(8,128)(2,1)} %bitcast.124), channel_id=1, source_target_pairs={{16,0},{32,16},{48,32},{64,48},{80,64},{96,80},{112,96},{128,112},... | collective-permute-start | bytes 393224 | tf_op jit(solution)/shard_map/while/body/eval_jaxpr/ppermute | solution.py:13
  552.3 17.1 %collective-permute-start = (bf16[64,1024]{1,0:T(8,128)(2,1)}, bf16[64,1024]{1,0:T(8,128)(2,1)S(1)}, u32[]{:S(2)}, u32[]{:S(2)}) collective-permute-start(bf16[64,1024]{1,0:T(8,128)(2,1)} %bitcast.124), channel_id=1, source_target_pairs={{16,0},{32,16},{48,32},{64,48},{80,64},{96,80},{112,96},{128,112},... | collective-permute-start | bytes 393224 | tf_op jit(solution)/shard_map/while/body/eval_jaxpr/ppermute | solution.py:13
  570.9 6.5 collective-permute-start
  577.4 12.6 %copy-start.9 = (f32[128,512]{1,0:T(8,128)S(1)}, f32[128,512]{1,0:T(8,128)}, u32[]{:S(2)}) copy-start(f32[128,512]{1,0:T(8,128)} %copy-done.8) | copy-start | bytes 786436
  578.3 77.8 %copy-start.7 = (f32[128,512]{1,0:T(8,128)S(1)}, f32[128,512]{1,0:T(8,128)}, u32[]{:S(2)}) copy-start(f32[128,512]{1,0:T(8,128)} %copy-done.6) | copy-start | bytes 786436
  592.5 107.7 %all-gather.31.cloned.1.call-start = ((), (), s32[]{:S(2)}) async-start(), calls=%async_computation.8 | async-start | bytes 1572864 | tf_op jit(solution)/shard_map/all_gather | solution.py:55
  658.8 88.0 %all-gather.33.cloned.1.call-start = ((), (), s32[]{:S(2)}) async-start(), calls=%async_computation.9 | async-start | bytes 1572864 | tf_op jit(solution)/shard_map/all_gather | solution.py:55
  700.2 49.5 %copy-start.4 = (bf16[4,128,1024]{2,1,0:T(8,128)(2,1)S(1)}, bf16[4,128,1024]{2,1,0:T(8,128)(2,1)}, u32[]{:S(2)}) copy-start(bf16[4,128,1024]{2,1,0:T(8,128)(2,1)} %param.10) | copy-start | bytes 3145732
  705.3 115.4 %reduce-scatter.4.cloned.1.call-start = ((), (), s32[]{:S(2)}) async-start(), calls=%async_computation.10 | async-start | bytes 4718592
  766.5 1.0 copy-start.2
  766.5 1.2 copy-start.10
Sparse Core Ops, SparseCore 0:
  10.1 62.3 all-gather.16
  77.5 44.0 all-gather.20
  125.7 41.3 all-gather.22
  171.1 41.2 all-gather.24
  215.0 64.4 all-gather.18
  281.4 41.5 all-gather.26
  592.7 62.0 all-gather.28
  658.9 41.3 all-gather.30
  705.4 41.2 all-gather.32
  766.7 53.9 reduce-scatter.3
